TPU v7x, 32 devices: a whole 2x2x4 slice. The times are simulated.
32 devices in a mesh: seq: 2 (over z_hi), fsdp: 8 (over y, x, core), dp: 2 (over z_lo).
Axes of the slice: x: 2, y: 2, z: 4 (z_hi: 2, z_lo: 2; z = z_hi * 2 + z_lo), core: 2. Of those that a mesh axis runs over, the one named last changes fastest.
Arguments:
- images: bfloat16 [48, 584, 1024], P(('fsdp', 'dp'), 'seq'), may hold values from -6 to 6
- key_mask: int32 [48, 584], P(('fsdp', 'dp')), may hold values from 0 to 1, as said below
- out_grad: bfloat16 [48, 584, 1024], P(('fsdp', 'dp'), 'seq'), may hold values from -6 to 6
- step_count: int32 [], replicated, may hold values from 2 to 20
- in_weights: float32 [1024, 3072], P(('seq', 'fsdp')), may hold values from -0.25 to 0.25
- out_weights: float32 [1024, 1024], P(('seq', 'fsdp')), may hold values from -0.375 to 0.375
- up_weights: float32 [4096, 1024], P(('seq', 'fsdp')), may hold values from -0.1875 to 0.1875
- down_weights: float32 [4096, 1024], P(('seq', 'fsdp')), may hold values from -0.09375 to 0.09375
- vectors: float32 [12288], P(('seq', 'fsdp')), may hold values from -0.4 to 1.4
- first_in: float32 [1024, 3072], P(('seq', 'fsdp')), may hold values from -1.5 to 1.5
- first_out: float32 [1024, 1024], P(('seq', 'fsdp')), may hold values from -0.9 to 0.9
- first_up: float32 [4096, 1024], P(('seq', 'fsdp')), may hold values from -2.2 to 2.2
- first_down: float32 [4096, 1024], P(('seq', 'fsdp')), may hold values from -4.5 to 4.5
- first_vectors: float32 [12288], P(('seq', 'fsdp')), may hold values from -4.5 to 4.5
- second_in: float32 [1024, 3072], P(('seq', 'fsdp')), may hold values from 0.03 to 0.25
- second_out: float32 [1024, 1024], P(('seq', 'fsdp')), may hold values from 0.012 to 0.09
- second_up: float32 [4096, 1024], P(('seq', 'fsdp')), may hold values from 0.07 to 0.55
- second_down: float32 [4096, 1024], P(('seq', 'fsdp')), may hold values from 0.28 to 2.2
- second_vectors: float32 [12288], P(('seq', 'fsdp')), may hold values from 0.28 to 2.2
Outputs:
- grad_norm: float32 [], replicated
- new_in: float32 [1024, 3072], P(('seq', 'fsdp'))
- new_out: float32 [1024, 1024], P(('seq', 'fsdp'))
- new_up: float32 [4096, 1024], P(('seq', 'fsdp'))
- new_down: float32 [4096, 1024], P(('seq', 'fsdp'))
- new_vectors: float32 [12288], P(('seq', 'fsdp'))
- first_in_new: float32 [1024, 3072], P(('seq', 'fsdp'))
- first_out_new: float32 [1024, 1024], P(('seq', 'fsdp'))
- first_up_new: float32 [4096, 1024], P(('seq', 'fsdp'))
- first_down_new: float32 [4096, 1024], P(('seq', 'fsdp'))
- first_vectors_new: float32 [12288], P(('seq', 'fsdp'))
- second_in_new: float32 [1024, 3072], P(('seq', 'fsdp'))
- second_out_new: float32 [1024, 1024], P(('seq', 'fsdp'))
- second_up_new: float32 [4096, 1024], P(('seq', 'fsdp'))
- second_down_new: float32 [4096, 1024], P(('seq', 'fsdp'))
- second_vectors_new: float32 [12288], P(('seq', 'fsdp'))
- copy_in: bfloat16 [1024, 3072], P(('seq', 'fsdp'))
- copy_out: bfloat16 [1024, 1024], P(('seq', 'fsdp'))
- copy_up: bfloat16 [4096, 1024], P(('seq', 'fsdp'))
- copy_down: bfloat16 [4096, 1024], P(('seq', 'fsdp'))
- copy_vectors: bfloat16 [12288], P(('seq', 'fsdp'))
- activations: float32 [48, 584, 1024], P(('fsdp', 'dp'), 'seq')
- input_grad: float32 [48, 584, 1024], P(('fsdp', 'dp'), 'seq')
Inputs may be any that keep to these rules, and one draw needn't show every extreme that they name: `key_mask`: every image has exactly 577 ones; where its 7 zeros stand is drawn afresh for each image.
All inputs are finite; a program needn't handle non-finite values.
Results may differ from a plain program's by a relative error of at most 0.02.
The roundings to bfloat16 on the way count: a program that leaves them out, or rounds other values in their place, can miss the bound.
Values may be sent and summed in bfloat16 or wider, within the bound.
A program may use at most 256 MiB of HBM per device.

v0:
```python
import math
import jax
import jax.numpy as jnp
from jax import lax
from jax.sharding import PartitionSpec as P

D = 1024
HD = 64
FF = 4096
NEG_FILL = -1000000000.0
NORM_EPS = 1e-06
ADAM_EPS = 1e-08
WEIGHT_DECAY = 0.05


def layer_norm(values, norm_gain, norm_shift):
    center = values - jnp.mean(values, axis=-1, keepdims=True)
    spread = jnp.mean(center * center, axis=-1, keepdims=True)
    return center * lax.rsqrt(spread + NORM_EPS) * norm_gain + norm_shift


def gelu_tanh(values):
    return jax.nn.gelu(values, approximate=True)


def matmul(former, latter):
    return jnp.dot(former, latter, preferred_element_type=jnp.float32)


def by_rows(former, latter):
    return lax.dot_general(
        former, latter, (((0,), (0,)), ((), ())), preferred_element_type=jnp.float32
    )


def by_columns(former, latter):
    return lax.dot_general(
        former, latter, (((1,), (1,)), ((), ())), preferred_element_type=jnp.float32
    )


def split_heads(head_block):
    token_count = head_block.shape[0]
    local_heads = head_block.shape[2] // HD
    queries = head_block[:, 0].reshape(token_count, local_heads, HD)
    key_rows = head_block[:, 1].reshape(token_count, local_heads, HD)
    value_rows = head_block[:, 2].reshape(token_count, local_heads, HD)
    return (queries, key_rows, value_rows)


def masked_scores(queries, key_rows, mask_row):
    scores = jnp.einsum(
        "qhd,khd->hqk", queries, key_rows, preferred_element_type=jnp.float32
    ) * HD ** (-0.5)
    return jnp.where((mask_row > 0)[None, None, :], scores, NEG_FILL)


def attend_image(packed_item):
    head_block, mask_row = packed_item
    queries, key_rows, value_rows = split_heads(head_block)
    scores = masked_scores(queries, key_rows, mask_row)
    row_max = jnp.max(scores, axis=-1, keepdims=True)
    exponent = jnp.exp(scores - row_max)
    row_total = jnp.sum(exponent, axis=-1, keepdims=True)
    attention = (exponent / row_total).astype(jnp.bfloat16)
    log_totals = (row_max + jnp.log(row_total))[..., 0]
    mixed = jnp.einsum("hqk,khd->qhd", attention, value_rows, preferred_element_type=jnp.float32)
    token_count = head_block.shape[0]
    return (mixed.reshape(token_count, head_block.shape[2]).astype(jnp.bfloat16), log_totals)


def attend_back(packed_item):
    head_block, log_totals, mask_row, grad_mixed = packed_item
    queries, key_rows, value_rows = split_heads(head_block)
    token_count = head_block.shape[0]
    local_heads = head_block.shape[2] // HD
    scores = masked_scores(queries, key_rows, mask_row)
    attention = jnp.exp(scores - log_totals[..., None])
    grad_view = grad_mixed.reshape(token_count, local_heads, HD)
    grad_attention = jnp.einsum(
        "qhd,khd->hqk", grad_view, value_rows, preferred_element_type=jnp.float32
    )
    row_delta = jnp.sum(attention * grad_attention, axis=-1, keepdims=True)
    grad_scores = jnp.where(
        (mask_row > 0)[None, None, :], attention * (grad_attention - row_delta), 0.0
    ).astype(jnp.bfloat16)
    grad_queries = jnp.einsum(
        "hqk,khd->qhd", grad_scores, key_rows, preferred_element_type=jnp.float32
    ) * HD ** (-0.5)
    grad_keys = jnp.einsum(
        "hqk,qhd->khd", grad_scores, queries, preferred_element_type=jnp.float32
    ) * HD ** (-0.5)
    grad_values = jnp.einsum(
        "hqk,qhd->khd",
        attention.astype(jnp.bfloat16),
        grad_view,
        preferred_element_type=jnp.float32,
    )
    stacked = jnp.stack([grad_queries, grad_keys, grad_values], axis=1)
    return stacked.reshape(token_count, 3, head_block.shape[2]).astype(jnp.bfloat16)


def adam_update(master, first_moment, second_moment, gradient, step_rate, bias_one, bias_two):
    first_new = 0.5 * first_moment + 0.5 * gradient
    second_new = 0.5 * second_moment + 0.5 * gradient * gradient
    update = first_new / bias_one / (jnp.sqrt(second_new / bias_two) + ADAM_EPS)
    master_new = master - step_rate * (update + WEIGHT_DECAY * master)
    return (master_new, first_new, second_new)


def on_device(
    images,
    key_mask,
    out_grad,
    step_count,
    in_weights,
    out_weights,
    up_weights,
    down_weights,
    vectors,
    first_in,
    first_out,
    first_up,
    first_down,
    first_vectors,
    second_in,
    second_out,
    second_up,
    second_down,
    second_vectors,
):
    full_in, full_out, full_vec = (
        lax.all_gather(in_weights.astype(jnp.bfloat16), ("seq", "fsdp"), axis=0, tiled=True),
        lax.all_gather(out_weights.astype(jnp.bfloat16), ("seq", "fsdp"), axis=0, tiled=True),
        lax.all_gather(vectors.astype(jnp.bfloat16), ("seq", "fsdp"), axis=0, tiled=True),
    )
    full_up, full_down = (
        lax.all_gather(up_weights.astype(jnp.bfloat16), ("seq", "fsdp"), axis=0, tiled=True),
        lax.all_gather(down_weights.astype(jnp.bfloat16), ("seq", "fsdp"), axis=0, tiled=True),
    )
    image_count, half_tokens, features = images.shape
    row_count = image_count * half_tokens
    vector_copy = full_vec.astype(jnp.float32)
    gain_one = vector_copy[0:features]
    shift_one = vector_copy[features : 2 * features]
    query_bias = vector_copy[2 * features : 3 * features]
    value_bias = vector_copy[3 * features : 4 * features]
    out_bias = vector_copy[4 * features : 5 * features]
    gain_two = vector_copy[5 * features : 6 * features]
    shift_two = vector_copy[6 * features : 7 * features]
    down_bias = vector_copy[7 * features : 8 * features]
    up_bias = vector_copy[8 * features :]
    in_bias = jnp.concatenate([query_bias, jnp.zeros_like(query_bias), value_bias])
    flat_input = images.reshape(row_count, features).astype(jnp.float32)
    normed_one = layer_norm(flat_input, gain_one, shift_one).astype(jnp.bfloat16)
    packed = (matmul(normed_one, full_in) + in_bias).astype(jnp.bfloat16)
    packed = packed.reshape(image_count, half_tokens, 3, features)
    head_packed = lax.all_to_all(packed, "seq", split_axis=3, concat_axis=1, tiled=True)
    mixed_heads, log_totals = lax.map(attend_image, (head_packed, key_mask))
    mixed = lax.all_to_all(mixed_heads, "seq", split_axis=1, concat_axis=2, tiled=True).reshape(
        row_count, features
    )
    middle = flat_input + matmul(mixed, full_out) + out_bias
    normed_two = layer_norm(middle, gain_two, shift_two).astype(jnp.bfloat16)
    grad_result = out_grad.reshape(row_count, features)
    grad_result_wide = grad_result.astype(jnp.float32)
    grad_down_b = jnp.sum(grad_result_wide, axis=0)
    hidden_input = by_columns(normed_two, full_up) + up_bias
    hidden = gelu_tanh(hidden_input).astype(jnp.bfloat16)
    result = middle + matmul(hidden, full_down) + down_bias
    grad_down_w = by_rows(hidden, grad_result)
    grad_hidden = by_columns(grad_result, full_down)
    unused_value, gelu_back = jax.vjp(gelu_tanh, hidden_input)
    grad_hidden_in = gelu_back(grad_hidden)[0].astype(jnp.bfloat16)
    grad_up_b = jnp.sum(grad_hidden_in.astype(jnp.float32), axis=0)
    grad_up_w = by_rows(grad_hidden_in, normed_two)
    grad_normed_two = matmul(grad_hidden_in, full_up)
    unused_two, norm_back_two = jax.vjp(layer_norm, middle, gain_two, shift_two)
    grad_middle_norm, grad_gain_two, grad_shift_two = norm_back_two(grad_normed_two)
    grad_middle = grad_result_wide + grad_middle_norm
    grad_branch = grad_middle.astype(jnp.bfloat16)
    grad_out_b = jnp.sum(grad_branch.astype(jnp.float32), axis=0)
    grad_out_w = by_rows(mixed, grad_branch)
    grad_mixed = (
        by_columns(grad_branch, full_out)
        .astype(jnp.bfloat16)
        .reshape(image_count, half_tokens, features)
    )
    grad_heads = lax.all_to_all(grad_mixed, "seq", split_axis=2, concat_axis=1, tiled=True)
    grad_packed_heads = lax.map(attend_back, (head_packed, log_totals, key_mask, grad_heads))
    grad_packed = lax.all_to_all(
        grad_packed_heads, "seq", split_axis=1, concat_axis=3, tiled=True
    ).reshape(row_count, 3 * features)
    grad_in_w = by_rows(normed_one, grad_packed)
    column_sums = jnp.sum(grad_packed.astype(jnp.float32), axis=0)
    grad_query_b = column_sums[0:features]
    grad_value_b = column_sums[2 * features :]
    grad_normed_one = by_columns(grad_packed, full_in)
    unused_one, norm_back_one = jax.vjp(layer_norm, flat_input, gain_one, shift_one)
    grad_input_norm, grad_gain_one, grad_shift_one = norm_back_one(grad_normed_one)
    input_grad = grad_middle + grad_input_norm
    grad_vec = jnp.concatenate(
        [
            grad_gain_one,
            grad_shift_one,
            grad_query_b,
            grad_value_b,
            grad_out_b,
            grad_gain_two,
            grad_shift_two,
            grad_down_b,
            grad_up_b,
        ]
    )
    share_in, share_out, share_vec = (
        lax.psum_scatter(grad_in_w, ("seq", "fsdp"), scatter_dimension=0, tiled=True),
        lax.psum_scatter(grad_out_w, ("seq", "fsdp"), scatter_dimension=0, tiled=True),
        lax.psum_scatter(grad_vec, ("seq", "fsdp"), scatter_dimension=0, tiled=True),
    )
    share_up, share_down = (
        lax.psum_scatter(grad_up_w, ("seq", "fsdp"), scatter_dimension=0, tiled=True),
        lax.psum_scatter(grad_down_w, ("seq", "fsdp"), scatter_dimension=0, tiled=True),
    )
    share_in, share_out, share_up, share_down, share_vec = (
        lax.psum(share_in.astype(jnp.bfloat16), "dp").astype(jnp.float32),
        lax.psum(share_out.astype(jnp.bfloat16), "dp").astype(jnp.float32),
        lax.psum(share_up.astype(jnp.bfloat16), "dp").astype(jnp.float32),
        lax.psum(share_down.astype(jnp.bfloat16), "dp").astype(jnp.float32),
        lax.psum(share_vec.astype(jnp.bfloat16), "dp").astype(jnp.float32),
    )
    shares = (share_in, share_out, share_up, share_down, share_vec)
    square_part = (
        jnp.sum(share_in * share_in)
        + jnp.sum(share_out * share_out)
        + jnp.sum(share_up * share_up)
        + jnp.sum(share_down * share_down)
        + jnp.sum(share_vec * share_vec)
    )
    square_total = lax.psum(square_part, ("seq", "fsdp"))
    grad_norm = jnp.sqrt(square_total)
    threshold = 0.5 * math.sqrt(4 * D * D + 2 * D * FF + 12 * D)
    clip_factor = jnp.minimum(1.0, threshold / grad_norm)
    decay_power = jnp.power(jnp.float32(0.5), step_count.astype(jnp.float32))
    bias_one = 1.0 - decay_power
    bias_two = 1.0 - decay_power
    rates = ((D // 2) ** (-0.5), (D // 4) ** (-0.5), D ** (-0.5), FF ** (-0.5), 0.2)
    masters = (in_weights, out_weights, up_weights, down_weights, vectors)
    firsts = (first_in, first_out, first_up, first_down, first_vectors)
    seconds = (second_in, second_out, second_up, second_down, second_vectors)
    results = [
        adam_update(
            masters[index],
            firsts[index],
            seconds[index],
            shares[index] * clip_factor,
            rates[index],
            bias_one,
            bias_two,
        )
        for index in range(5)
    ]
    new_masters = [entry[0] for entry in results]
    new_firsts = [entry[1] for entry in results]
    new_seconds = [entry[2] for entry in results]
    copies = [master.astype(jnp.bfloat16) for master in new_masters]
    activations = result.reshape(image_count, half_tokens, features)
    input_grad = input_grad.reshape(image_count, half_tokens, features)
    return (
        grad_norm,
        new_masters[0],
        new_masters[1],
        new_masters[2],
        new_masters[3],
        new_masters[4],
        new_firsts[0],
        new_firsts[1],
        new_firsts[2],
        new_firsts[3],
        new_firsts[4],
        new_seconds[0],
        new_seconds[1],
        new_seconds[2],
        new_seconds[3],
        new_seconds[4],
        copies[0],
        copies[1],
        copies[2],
        copies[3],
        copies[4],
        activations,
        input_grad,
    )


def solution(mesh):
    placed = (
        P(("fsdp", "dp"), "seq", None),
        P(("fsdp", "dp"), None),
        P(("fsdp", "dp"), "seq", None),
        P(),
        P(("seq", "fsdp"), None),
        P(("seq", "fsdp"), None),
        P(("seq", "fsdp"), None),
        P(("seq", "fsdp"), None),
        P(("seq", "fsdp")),
        P(("seq", "fsdp"), None),
        P(("seq", "fsdp"), None),
        P(("seq", "fsdp"), None),
        P(("seq", "fsdp"), None),
        P(("seq", "fsdp")),
        P(("seq", "fsdp"), None),
        P(("seq", "fsdp"), None),
        P(("seq", "fsdp"), None),
        P(("seq", "fsdp"), None),
        P(("seq", "fsdp")),
    )
    return jax.shard_map(
        on_device,
        mesh=mesh,
        in_specs=placed,
        out_specs=(
            P(),
            P(("seq", "fsdp"), None),
            P(("seq", "fsdp"), None),
            P(("seq", "fsdp"), None),
            P(("seq", "fsdp"), None),
            P(("seq", "fsdp")),
            P(("seq", "fsdp"), None),
            P(("seq", "fsdp"), None),
            P(("seq", "fsdp"), None),
            P(("seq", "fsdp"), None),
            P(("seq", "fsdp")),
            P(("seq", "fsdp"), None),
            P(("seq", "fsdp"), None),
            P(("seq", "fsdp"), None),
            P(("seq", "fsdp"), None),
            P(("seq", "fsdp")),
            P(("seq", "fsdp"), None),
            P(("seq", "fsdp"), None),
            P(("seq", "fsdp"), None),
            P(("seq", "fsdp"), None),
            P(("seq", "fsdp")),
            P(("fsdp", "dp"), "seq", None),
            P(("fsdp", "dp"), "seq", None),
        ),
        check_vma=False,
    )
```

profile of v0, /device:TPU:0, one launch (start us, length us, event | category | flops | bytes accessed | tf_op | source)
XLA Modules:
  0.0 1772.8 jit_solution(14183998428511871880)
XLA Ops:
  17.8 23.3 %all-gather = bf16[16,1,768]{2,1,0:T(2,128)(2,1)S(1)} all-gather(bf16[1,1,768]{2,1,0:T(2,128)(2,1)S(1)} %reshape.302), channel_id=1, replica_groups=mesh['seq'=2,'fsdp'=8,'dp'=2] {'seq','fsdp'}, dimensions={0}, use_global_device_ids=true | all-gather | bytes 26112 | tf_op jit(solution)/shard_map/all_gather | solution.py:135
  42.4 39.8 %all-gather.6.cloned.1.call-done = bf16[1024,3072]{1,0:T(8,128)(2,1)} async-done(((bf16[64,3072]{1,0:T(8,128)(2,1)}), bf16[1024,3072]{1,0:T(8,128)(2,1)}) %all-gather.6.cloned.1.call-update) | async-done | bytes 6291472 | tf_op jit(solution)/shard_map/all_gather | solution.py:133
  82.2 11.2 add_convert_fusion
  93.5 16.3 reshape.294
  109.8 18.0 %copy.98 = bf16[3,292,3,1024]{1,2,0,3:T(4,128)(2,1)} copy(bf16[3,292,3,1024]{3,2,1,0:T(4,128)(2,1)} %reshape.294) | data formatting | bytes 10764288 | tf_op jit(solution)/shard_map/reshape | solution.py:157
  127.8 7.5 all-to-all-start
  136.5 308.5 %all-to-all-done = bf16[3,292,3,1024]{1,2,0,3:T(4,128)(2,1)} async-done(((bf16[3,292,3,1024]{1,2,0,3:T(4,128)(2,1)}), bf16[3,292,3,1024]{1,2,0,3:T(4,128)(2,1)}, u32[]{:S(2)}, u32[]{:S(2)}) %all-to-all-start) | async-done | bytes 5382176 | tf_op jit(solution)/shard_map/all_to_all | solution.py:158
  445.0 14.7 copy.135
  459.7 14.5 reshape.307
  474.2 32.3 %while.22 = (s32[]{:T(128)}, bf16[3,584,512]{1,2,0:T(8,128)(2,1)S(1)}, f32[3,8,584]{2,1,0:T(8,128)S(1)}, bf16[3,584,3,512]{1,3,2,0:T(8,128)(2,1)}, s32[3,584]{1,0:T(4,128)S(1)}, /*index=5*/s32[]{:T(128)}) while((s32[]{:T(128)}, bf16[3,584,512]{1,2,0:T(8,128)(2,1)S(1)}, f32[3,8,584]{2,1,0:T(8,128)S(1)}, bf16[3,584,3,512]{1,3,2,0:T(8,128)(2,1)}, ...), condition=%wide.region_5.6_spmd, body=%wide.region_2.5_spmd.sunk | while | flops 731518976 | bytes 43779996 | solution.py:159
  481.5 3.3 fusion.172
  486.9 2.8 fusion.170
  492.3 3.3 fusion.172
  497.7 2.8 fusion.170
  503.1 3.3 fusion.172
  506.5 3.7 copy.102
  510.2 5.4 all-to-all-start.1
  518.0 43.1 %all-to-all-done.1 = bf16[3,584,512]{2,0,1:T(4,128)(2,1)} async-done(((bf16[3,584,512]{2,0,1:T(4,128)(2,1)}), bf16[3,584,512]{2,0,1:T(4,128)(2,1)}, u32[]{:S(2)}, u32[]{:S(2)}) %all-to-all-start.1) | async-done | bytes 1794080 | tf_op jit(solution)/shard_map/all_to_all | solution.py:160
  567.7 5.3 fusion.109
  575.4 15.2 fusion.90
  590.5 22.0 %convert_reduce_fusion = (f32[4096]{0:T(1024)}, bf16[876,4096]{1,0:T(8,128)(2,1)}) fusion(f32[876,4096]{1,0:T(8,128)} %fusion.90, f32[4096]{0:T(1024)S(1)} %slice.83, bf16[876,1024]{1,0:T(8,128)(2,1)S(1)} %reshape.295, bf16[4096,1024]{1,0:T(8,128)(2,1)} %all-gather.8.cloned.1.call-done), kind=kOutput, calls=%fused_computation.60 | convolution fusion | flops 7430942720 | bytes 31744000 | tf_op jit(solution)/shard_map/dot_general | solution.py:37
  612.6 13.6 multiply_reduce_fusion.3
  631.7 3.3 convolution_convert_fusion
  636.6 3.9 copy.105
  640.5 3.9 all-to-all-start.2
  644.5 6.4 fusion.113
  651.0 89.5 %all-to-all-done.2 = bf16[3,292,1024]{1,0,2:T(4,128)(2,1)S(1)} async-done(((bf16[3,292,1024]{1,0,2:T(4,128)(2,1)}), bf16[3,292,1024]{1,0,2:T(4,128)(2,1)S(1)}, u32[]{:S(2)}, u32[]{:S(2)}) %all-to-all-start.2) | async-done | bytes 1794080 | tf_op jit(solution)/shard_map/all_to_all | solution.py:189
  740.5 4.2 copy.136
  744.7 5.8 reshape.305
  750.5 183.9 %while.23 = (s32[]{:T(128)}, bf16[3,584,3,512]{1,3,2,0:T(8,128)(2,1)}, bf16[3,584,3,512]{1,3,2,0:T(8,128)(2,1)}, s32[3,584]{1,0:T(4,128)S(1)}, f32[3,8,584]{2,1,...) while((s32[]{:T(128)}, bf16[3,584,3,512]{1,3,2,0:T(8,128)(2,1)}, ...), condition=%wide.region_12.13_spmd, body=%wide.region_10.12_spmd.sunk | while | flops 1824034688 | bytes 138262480 | solution.py:190
  756.1 2.8 fusion.185
  760.4 6.4 fusion.186
  766.8 21.8 %fusion.188 = bf16[8,64,584]{2,1,0:T(8,128)(2,1)S(1)} fusion(bf16[584,8,64]{0,2,1:T(8,128)(2,1)S(1)} %bitcast.145, f32[8,584,584]{1,2,0:T(8,128)} %fusion.186, f32[8,584,584]{1,2,0:T(8,128)} %copy-done, f32[8,584]{1,0:T(8,128)S(1)} %dynamic-slice_bitcast_fusion.8, pred[584]{0:T(1024)(128)(4,1)S(1)} %compare_reduce_fusion.5), kind=kOutput, calls=%fused_computation.38.clone.1 | convolution fusion | flops 379857536 | bytes 23042888 | tf_op jit(solution)/shard_map/while/body/eval_jaxpr/hqk,khd->qhd/dot_general | solution.py:87
  788.6 21.9 %fusion.187 = bf16[8,64,584]{2,1,0:T(8,128)(2,1)S(1)} fusion(bf16[584,8,64]{0,2,1:T(8,128)(2,1)S(1)} %bitcast.143, f32[8,584,584]{1,2,0:T(8,128)} %fusion.186, f32[8,584,584]{1,2,0:T(8,128)} %copy-done, f32[8,584]{1,0:T(8,128)S(1)} %dynamic-slice_bitcast_fusion.8, pred[584]{0:T(1024)(128)(4,1)S(1)} %compare_reduce_fusion.5), kind=kOutput, calls=%fused_computation.37.clone.1 | convolution fusion | flops 379857536 | bytes 23042888 | tf_op jit(solution)/shard_map/while/body/eval_jaxpr/hqk,qhd->khd/dot_general | solution.py:90
  817.2 2.8 fusion.185
  821.6 6.4 fusion.186
  827.9 21.8 %fusion.188 = bf16[8,64,584]{2,1,0:T(8,128)(2,1)S(1)} fusion(bf16[584,8,64]{0,2,1:T(8,128)(2,1)S(1)} %bitcast.145, f32[8,584,584]{1,2,0:T(8,128)} %fusion.186, f32[8,584,584]{1,2,0:T(8,128)} %copy-done, f32[8,584]{1,0:T(8,128)S(1)} %dynamic-slice_bitcast_fusion.8, pred[584]{0:T(1024)(128)(4,1)S(1)} %compare_reduce_fusion.5), kind=kOutput, calls=%fused_computation.38.clone.1 | convolution fusion | flops 379857536 | bytes 23042888 | tf_op jit(solution)/shard_map/while/body/eval_jaxpr/hqk,khd->qhd/dot_general | solution.py:87
  849.8 21.9 %fusion.187 = bf16[8,64,584]{2,1,0:T(8,128)(2,1)S(1)} fusion(bf16[584,8,64]{0,2,1:T(8,128)(2,1)S(1)} %bitcast.143, f32[8,584,584]{1,2,0:T(8,128)} %fusion.186, f32[8,584,584]{1,2,0:T(8,128)} %copy-done, f32[8,584]{1,0:T(8,128)S(1)} %dynamic-slice_bitcast_fusion.8, pred[584]{0:T(1024)(128)(4,1)S(1)} %compare_reduce_fusion.5), kind=kOutput, calls=%fused_computation.37.clone.1 | convolution fusion | flops 379857536 | bytes 23042888 | tf_op jit(solution)/shard_map/while/body/eval_jaxpr/hqk,qhd->khd/dot_general | solution.py:90
  878.3 2.8 fusion.185
  882.7 6.4 fusion.186
  889.0 21.8 %fusion.188 = bf16[8,64,584]{2,1,0:T(8,128)(2,1)S(1)} fusion(bf16[584,8,64]{0,2,1:T(8,128)(2,1)S(1)} %bitcast.145, f32[8,584,584]{1,2,0:T(8,128)} %fusion.186, f32[8,584,584]{1,2,0:T(8,128)} %copy-done, f32[8,584]{1,0:T(8,128)S(1)} %dynamic-slice_bitcast_fusion.8, pred[584]{0:T(1024)(128)(4,1)S(1)} %compare_reduce_fusion.5), kind=kOutput, calls=%fused_computation.38.clone.1 | convolution fusion | flops 379857536 | bytes 23042888 | tf_op jit(solution)/shard_map/while/body/eval_jaxpr/hqk,khd->qhd/dot_general | solution.py:87
  910.9 21.9 %fusion.187 = bf16[8,64,584]{2,1,0:T(8,128)(2,1)S(1)} fusion(bf16[584,8,64]{0,2,1:T(8,128)(2,1)S(1)} %bitcast.143, f32[8,584,584]{1,2,0:T(8,128)} %fusion.186, f32[8,584,584]{1,2,0:T(8,128)} %copy-done, f32[8,584]{1,0:T(8,128)S(1)} %dynamic-slice_bitcast_fusion.8, pred[584]{0:T(1024)(128)(4,1)S(1)} %compare_reduce_fusion.5), kind=kOutput, calls=%fused_computation.37.clone.1 | convolution fusion | flops 379857536 | bytes 23042888 | tf_op jit(solution)/shard_map/while/body/eval_jaxpr/hqk,qhd->khd/dot_general | solution.py:90
  934.4 13.4 copy.110
  947.8 6.7 all-to-all-start.3
  958.2 143.0 %all-to-all-done.3 = bf16[3,584,3,512]{3,2,0,1:T(4,128)(2,1)} async-done(((bf16[3,584,3,512]{3,2,0,1:T(4,128)(2,1)}), bf16[3,584,3,512]{3,2,0,1:T(4,128)(2,1)}, u32[]{:S(2)}, u32[]{:S(2)}) %all-to-all-start.3) | async-done | bytes 5382176 | tf_op jit(solution)/shard_map/all_to_all | solution.py:191
  1101.2 4.6 convert_reduce_fusion.1
  1105.8 9.6 copy.112
  1115.5 12.9 reshape.298
  1128.4 12.1 fusion.112
  1142.0 18.8 %fusion.91 = f32[4096,1024]{1,0:T(8,128)} fusion(bf16[876,1024]{1,0:T(8,128)(2,1)S(1)} %copy-done.6, f32[876,4096]{1,0:T(8,128)} %fusion.90, f32[4096]{0:T(1024)S(1)} %copy-done.45), kind=kOutput, calls=%fused_computation.152 | convolution fusion | flops 7384301568 | bytes 32940032 | tf_op jit(solution)/shard_map/dot_general | solution.py:31
  1161.6 17.9 %fusion.89 = f32[4096,1024]{1,0:T(8,128)} fusion(bf16[876,4096]{1,0:T(8,128)(2,1)} %get-tuple-element.185, f32[876,1024]{1,0:T(8,128)} %copy-done.7, f32[1024]{0:T(1024)S(1)} %copy-done.51, f32[1024]{0:T(1024)S(1)} %copy-done.35, f32[876]{0:T(1024)S(1)} %copy-done.41, f32[876]{0:T(1024)S(1)} %copy-done.26), kind=kOutput, calls=%fused_computation.150 | convolution fusion | flops 7352905728 | bytes 27556704 | tf_op jit(solution)/shard_map/dot_general | solution.py:31
  1183.3 17.0 add_add_fusion.3
  1200.3 3.8 reshape.299
  1204.1 12.4 multiply_reduce_fusion.2
  1216.7 72.3 %all-reduce = bf16[12288]{0:T(1024)(128)(2,1)S(1)} all-reduce(f32[12288]{0:T(1024)S(1)} %constant_dynamic-update-slice_fusion.1), channel_id=6, replica_groups=mesh['seq'=2,'fsdp'=8,'dp'=2] {'seq','fsdp'}, use_global_device_ids=true, to_apply=%region_33.34.clone | all-reduce | flops 12288 | bytes 73728
  1289.0 4.9 psum.46
  1297.4 163.8 %reduce-scatter.11.cloned.1.call-done = f32[256,1024]{1,0:T(8,128)} async-done(((f32[4096,1024]{1,0:T(8,128)}), f32[256,1024]{1,0:T(8,128)}) %reduce-scatter.11.cloned.1.call-update) | async-done | bytes 1048592 | tf_op jit(solution)/shard_map/reduce_scatter | solution.py:222
  1463.3 183.6 %reduce-scatter.9.cloned.1.call-done = f32[256,1024]{1,0:T(8,128)} async-done(((f32[4096,1024]{1,0:T(8,128)}), f32[256,1024]{1,0:T(8,128)}) %reduce-scatter.9.cloned.1.call-update) | async-done | bytes 1048592 | tf_op jit(solution)/shard_map/reduce_scatter | solution.py:221
  1649.7 4.3 fusion.92
  1656.6 48.6 %all-reduce.4.cloned.1.call-done = (bf16[64,3072]{1,0:T(8,128)(2,1)}, bf16[64,1024]{1,0:T(8,128)(2,1)}, bf16[256,1024]{1,0:T(8,128)(2,1)}, bf16[256,1024]{1,0:T(8,128)(2,1)}) async-done(((bf16[64,3072]{1,0:T(8,128)(2,1)}, bf16[64,1024]{1,0:T(8,128)(2,1)}, bf16[256,1024]{1,0:T(8,128)(2,1)}, bf16[256,1024]{1,0:T(8,128)(2,1)}), (bf16[64,3072]{1,0:T(8,128)(2,1)}, bf16[64,1024]{1,0:T(8,128)(2,1)}, ...) | async-done | bytes 1572880 | tf_op jit(solution)/shard_map/psum | solution.py:225
  1715.7 3.7 reshape.300
  1719.4 34.1 %psum.47 = f32[]{:T(128)} all-reduce(f32[]{:T(128)S(6)} %add.246), channel_id=1, replica_groups=mesh['seq'=2,'fsdp'=8,'dp'=2] {'seq','fsdp'}, use_global_device_ids=true, to_apply=%region_36.37 | all-reduce | flops 1 | bytes 8 | tf_op jit(solution)/shard_map/psum | solution.py:239
  1757.4 3.5 fusion.101
  1761.0 3.7 fusion.95
  (251 shorter events, 102.2 us)
Async XLA Ops:
  7.2 6.7 copy-start.3
  7.2 75.0 %all-gather.6.cloned.1.call-start = ((), (), s32[]{:S(2)}) async-start(), calls=%async_computation.8 | async-start | bytes 6684672 | tf_op jit(solution)/shard_map/all_gather | solution.py:133
  9.3 558.3 %all-gather.10.cloned.1.call-start = ((), (), s32[]{:S(2)}) async-start(), calls=%async_computation.10 | async-start | bytes 2228224 | tf_op jit(solution)/shard_map/all_gather | solution.py:134
  11.0 564.3 %all-gather.12.cloned.1.call-start = ((), (), s32[]{:S(2)}) async-start(), calls=%async_computation.11 | async-start | bytes 8912896 | tf_op jit(solution)/shard_map/all_gather | solution.py:138
  16.4 77.1 %copy-start.22 = (f32[3,292]{1,0:T(4,128)}, f32[3,292]{1,0:T(4,128)S(1)}, u32[]{:S(2)}) copy-start(f32[3,292]{1,0:T(4,128)S(1)} %broadcast_multiply_fusion) | copy-start | bytes 10516
  16.5 77.0 %copy-start.36 = (f32[876]{0:T(1024)}, f32[876]{0:T(1024)S(1)}, u32[]{:S(2)}) copy-start(f32[876]{0:T(1024)S(1)} %div.108) | copy-start | bytes 10516
  17.8 23.4 %copy-start.31 = (f32[876]{0:T(1024)}, f32[876]{0:T(1024)S(1)}, u32[]{:S(2)}) copy-start(f32[876]{0:T(1024)S(1)} %add.227) | copy-start | bytes 10516
  17.8 75.7 %copy-start.38 = (f32[876]{0:T(1024)}, f32[876]{0:T(1024)S(1)}, u32[]{:S(2)}) copy-start(f32[876]{0:T(1024)S(1)} %rsqrt.26) | copy-start | bytes 10516
  42.4 51.1 %copy-start.27 = (f32[1024]{0:T(1024)}, f32[1024]{0:T(1024)S(1)}, u32[]{:S(2)}) copy-start(f32[1024]{0:T(1024)S(1)} %get-tuple-element.207) | copy-start | bytes 12292
  42.4 51.1 %copy-start.47 = (f32[1024]{0:T(1024)}, f32[1024]{0:T(1024)S(1)}, u32[]{:S(2)}) copy-start(f32[1024]{0:T(1024)S(1)} %get-tuple-element.206) | copy-start | bytes 12292
  127.8 7.7 copy-start.10
  127.8 317.2 %all-to-all-start = ((bf16[3,292,3,1024]{1,2,0,3:T(4,128)(2,1)}), bf16[3,292,3,1024]{1,2,0,3:T(4,128)(2,1)}, u32[]{:S(2)}, u32[]{:S(2)}) async-start(bf16[3,292,3,1024]{1,2,0,3:T(4,128)(2,1)} %copy.98), calls=%async_computation | async-start | bytes 18874368 | tf_op jit(solution)/shard_map/all_to_all | solution.py:158
  135.3 455.3 %all-gather.8.cloned.1.call-start = ((), (), s32[]{:S(2)}) async-start(), calls=%async_computation.9 | async-start | bytes 8912896 | tf_op jit(solution)/shard_map/all_gather | solution.py:139
  459.7 14.5 copy-start.24
  510.2 50.8 %all-to-all-start.1 = ((bf16[3,584,512]{2,0,1:T(4,128)(2,1)}), bf16[3,584,512]{2,0,1:T(4,128)(2,1)}, u32[]{:S(2)}, u32[]{:S(2)}) async-start(bf16[3,584,512]{2,0,1:T(4,128)(2,1)} %copy.102), calls=%async_computation.1 | async-start | bytes 4784128 | tf_op jit(solution)/shard_map/all_to_all | solution.py:160
  516.4 74.2 %copy-start.44 = (f32[4096]{0:T(1024)}, f32[4096]{0:T(1024)S(1)}, u32[]{:S(2)}) copy-start(f32[4096]{0:T(1024)S(1)} %slice.83) | copy-start | bytes 49156
  518.0 109.5 %copy-start.5 = (bf16[876,1024]{1,0:T(8,128)(2,1)}, bf16[876,1024]{1,0:T(8,128)(2,1)S(1)}, u32[]{:S(2)}) copy-start(bf16[876,1024]{1,0:T(8,128)(2,1)S(1)} %reshape.295) | copy-start | bytes 5382148
  563.2 4.5 copy-start.52
  567.6 7.7 copy-start.34
  567.7 7.7 copy-start.50
  573.0 53.2 %copy-start.25 = (f32[876]{0:T(1024)}, f32[876]{0:T(1024)S(1)}, u32[]{:S(2)}) copy-start(f32[876]{0:T(1024)S(1)} %broadcast_multiply_fusion.1) | copy-start | bytes 10516
  575.3 50.9 %copy-start.40 = (f32[876]{0:T(1024)}, f32[876]{0:T(1024)S(1)}, u32[]{:S(2)}) copy-start(f32[876]{0:T(1024)S(1)} %fusion.87) | copy-start | bytes 10516
  590.5 22.0 %copy-start.8 = (f32[876,1024]{1,0:T(8,128)S(1)}, f32[876,1024]{1,0:T(8,128)}, u32[]{:S(2)}) copy-start(f32[876,1024]{1,0:T(8,128)} %copy-done.7) | copy-start | bytes 10764292
  627.4 1.8 copy-start.1
  627.4 4.3 copy-start.57
  627.4 3.1 copy-start.29
  640.5 100.0 %all-to-all-start.2 = ((bf16[3,292,1024]{1,0,2:T(4,128)(2,1)}), bf16[3,292,1024]{1,0,2:T(4,128)(2,1)S(1)}, u32[]{:S(2)}, u32[]{:S(2)}) async-start(bf16[3,292,1024]{1,0,2:T(4,128)(2,1)} %copy.105), calls=%async_computation.2 | async-start | bytes 6291456 | tf_op jit(solution)/shard_map/all_to_all | solution.py:189
  644.5 649.4 %reduce-scatter.7.cloned.1.call-start = ((), (), s32[]{:S(2)}) async-start(), calls=%async_computation.13 | async-start | bytes 4456448 | tf_op jit(solution)/shard_map/reduce_scatter | solution.py:217
  756.0 4.4 copy-start
  817.2 4.4 copy-start
  878.3 4.4 copy-start
  947.8 6.8 copy-start.4
  947.8 6.8 copy-start.23
  947.8 6.8 copy-start.28
  947.8 6.8 copy-start.33
  947.8 6.8 copy-start.48
  947.8 153.4 %all-to-all-start.3 = ((bf16[3,584,3,512]{3,2,0,1:T(4,128)(2,1)}), bf16[3,584,3,512]{3,2,0,1:T(4,128)(2,1)}, u32[]{:S(2)}, u32[]{:S(2)}) async-start(bf16[3,584,3,512]{3,2,0,1:T(4,128)(2,1)} %copy.110), calls=%async_computation.3 | async-start | bytes 14352384 | tf_op jit(solution)/shard_map/all_to_all | solution.py:191
  954.5 341.0 %reduce-scatter.5.cloned.1.call-start = ((), (), s32[]{:S(2)}) async-start(), calls=%async_computation.12 | async-start | bytes 13369344 | tf_op jit(solution)/shard_map/reduce_scatter | solution.py:216
  1140.5 320.7 %reduce-scatter.11.cloned.1.call-start = ((), (), s32[]{:S(2)}) async-start(), calls=%async_computation.15 | async-start | bytes 17825792 | tf_op jit(solution)/shard_map/reduce_scatter | solution.py:222
  1160.8 486.1 %reduce-scatter.9.cloned.1.call-start = ((), (), s32[]{:S(2)}) async-start(), calls=%async_computation.14 | async-start | bytes 17825792 | tf_op jit(solution)/shard_map/reduce_scatter | solution.py:221
  1179.4 3.8 copy-start.49
  1179.5 525.7 %all-reduce.4.cloned.1.call-start = ((), (), s32[]{:S(2)}) async-start(), calls=%async_computation.16 | async-start | bytes 3145728 | tf_op jit(solution)/shard_map/psum | solution.py:225
  1200.3 3.8 copy-start.37
  1200.3 3.8 copy-start.39
  1204.0 12.5 copy-start.42
  1204.1 12.5 copy-start.54
  1204.1 12.5 copy-start.53
  1204.1 12.6 copy-start.43
  1216.5 433.1 %copy-start.32 = (f32[876]{0:T(1024)S(1)}, f32[876]{0:T(1024)}, u32[]{:S(2)}) copy-start(f32[876]{0:T(1024)} %copy-done.31) | copy-start | bytes 10516
  1649.6 4.3 copy-start.2
  1649.6 4.3 copy-start.30
  1656.5 97.7 %copy-start.46 = (f32[768]{0:T(1024)S(1)}, f32[768]{0:T(1024)}, u32[]{:S(2)}) copy-start(f32[768]{0:T(1024)} %param.31) | copy-start | bytes 9220
  1656.5 97.7 %copy-start.55 = (f32[768]{0:T(1024)S(1)}, f32[768]{0:T(1024)}, u32[]{:S(2)}) copy-start(f32[768]{0:T(1024)} %param.41) | copy-start | bytes 9220
  1656.5 97.7 %copy-start.56 = (f32[768]{0:T(1024)S(1)}, f32[768]{0:T(1024)}, u32[]{:S(2)}) copy-start(f32[768]{0:T(1024)} %param.36) | copy-start | bytes 9220
  1656.5 100.9 %copy-start.12 = (f32[64,3072]{1,0:T(8,128)S(1)}, f32[64,3072]{1,0:T(8,128)}, u32[]{:S(2)}) copy-start(f32[64,3072]{1,0:T(8,128)} %param.27) | copy-start | bytes 2359300
  1705.2 49.8 %copy-start.20 = (bf16[64,1024]{1,0:T(8,128)(2,1)S(1)}, bf16[64,1024]{1,0:T(8,128)(2,1)}, u32[]{:S(2)}) copy-start(bf16[64,1024]{1,0:T(8,128)(2,1)} %get-tuple-element.159) | copy-start | bytes 393220
  1719.4 41.5 %copy-start.9 = (f32[256,1024]{1,0:T(8,128)S(1)}, f32[256,1024]{1,0:T(8,128)}, u32[]{:S(2)}) copy-start(f32[256,1024]{1,0:T(8,128)} %param.29) | copy-start | bytes 3145732
  1719.4 41.5 %copy-start.11 = (f32[256,1024]{1,0:T(8,128)S(1)}, f32[256,1024]{1,0:T(8,128)}, u32[]{:S(2)}) copy-start(f32[256,1024]{1,0:T(8,128)} %param.30) | copy-start | bytes 3145732
  1719.4 41.6 %copy-start.13 = (bf16[256,1024]{1,0:T(8,128)(2,1)S(1)}, bf16[256,1024]{1,0:T(8,128)(2,1)}, u32[]{:S(2)}) copy-start(bf16[256,1024]{1,0:T(8,128)(2,1)} %get-tuple-element.160) | copy-start | bytes 1572868
  1754.3 6.7 copy-start.14
  1754.3 6.7 copy-start.16
  1754.3 6.7 copy-start.17
  1754.3 6.7 copy-start.18
  1754.3 6.7 copy-start.19
  (10 other events, 10.3 us)
Sparse Core Ops, SparseCore 0:
  10.9 71.2 all-gather.5
  85.1 40.6 all-gather.9
  128.7 207.7 all-gather.11
  339.3 107.4 all-gather.7
  651.1 106.3 reduce-scatter.6
  1140.6 138.3 reduce-scatter.4
  1281.4 179.7 reduce-scatter.10
  1463.6 183.2 reduce-scatter.8
  1650.2 54.9 all-reduce.3
where the time goes:
time: 1780 us; the launch traced here: 1770 us
  waiting for transfers between devices  1020 us (57%)
  matrix products  339 us (19%)
  local copies, waits for them, and re-layouts  168 us (9%)
  blocking collectives  135 us (8%)
  other arithmetic  65.3 us (4%)
  starting transfers between devices  24.1 us (1%)
  between operations  21.6 us (1%)
    all_to_all x1, waiting for transfers between devices, on_device(): lax.all_to_all(packed, 'seq', split_axis=3, concat_axis=1, tiled=True)  308 us
    reduce_scatter x1, waiting for transfers between devices, on_device(): lax.psum_scatter(grad_up_w, ('seq', 'fsdp'), scatter_dimension=0, tiled=T...  184 us
    reduce_scatter x1, waiting for transfers between devices, on_device(): lax.psum_scatter(grad_down_w, ('seq', 'fsdp'), scatter_dimension=0, tiled...  164 us
    all_to_all x1, waiting for transfers between devices, on_device(): lax.all_to_all(grad_packed_heads, 'seq', split_axis=1, concat_axis=3, til...  143 us
    all_to_all x1, waiting for transfers between devices, on_device(): lax.all_to_all(grad_mixed, 'seq', split_axis=2, concat_axis=1, tiled=True)  89.5 us
    unnamed x1, blocking collectives  72.3 us
    dot_general x3, matrix products, attend_back(): jnp.einsum('hqk,qhd->khd', grad_scores, queries, preferred_element_type=j...  65.8 us
    dot_general x3, matrix products, attend_back(): jnp.einsum('hqk,khd->qhd', grad_scores, key_rows, preferred_element_type=...  65.4 us
  transfers between devices with their start and end apart: 13, of which 8 were waited for; matrix products, arithmetic and copies ran while one was open for 27% of the time, Pallas kernels for 0%

commit v1 on v0

--- a/solution.py
+++ b/solution.py
@@ -1,3 +1,4 @@
+import functools
 import math
 import jax
 import jax.numpy as jnp
@@ -11,6 +12,14 @@
 NORM_EPS = 1e-06
 ADAM_EPS = 1e-08
 WEIGHT_DECAY = 0.05
+
+
+def _end_chains(own_rows, a_name):
+    passed = lax.all_gather(own_rows, a_name).sum(axis=0)
+    return passed
+
+
+map_bars = functools.partial(_end_chains, a_name="dp")
 
 
 def layer_norm(values, norm_gain, norm_shift):
@@ -222,7 +231,7 @@
         lax.psum_scatter(grad_down_w, ("seq", "fsdp"), scatter_dimension=0, tiled=True),
     )
     share_in, share_out, share_up, share_down, share_vec = (
-        lax.psum(share_in.astype(jnp.bfloat16), "dp").astype(jnp.float32),
+        map_bars(share_in.astype(jnp.bfloat16)).astype(jnp.float32),
         lax.psum(share_out.astype(jnp.bfloat16), "dp").astype(jnp.float32),
         lax.psum(share_up.astype(jnp.bfloat16), "dp").astype(jnp.float32),
         lax.psum(share_down.astype(jnp.bfloat16), "dp").astype(jnp.float32),

time: 1780 us -> 1540 us (0.87)
  waiting for transfers between devices: 1020 us -> 745 us
  blocking collectives: 135 us -> 164 us
    reduce_scatter x1, waiting for transfers between devices: 184 us -> 0.01 us  [on_device(): lax.psum_scatter(grad_up_w, ('seq', 'fsdp'), scatter_dimension=0, tiled=T...]
    reduce_scatter x1, waiting for transfers between devices: 164 us -> 0.01 us  [on_device(): lax.psum_scatter(grad_down_w, ('seq', 'fsdp'), scatter_dimension=0, tiled...]
    all_to_all x1, waiting for transfers between devices: 143 us -> 228 us  [on_device(): lax.all_to_all(grad_packed_heads, 'seq', split_axis=1, concat_axis=3, til...]
    psum x1, waiting for transfers between devices: 48.6 us -> 30.4 us  [on_device(): lax.psum(share_out.astype(jnp.bfloat16), 'dp').astype(jnp.float32)]
  transfers between devices with their start and end apart: 13 -> 13, of which waited for: 8 -> 7; matrix products, arithmetic and copies ran while one was open for 27% -> 33% of each run, Pallas kernels for 0% -> 0%
where the time goes in v1:
time: 1540 us; the launch traced here: 1530 us
  waiting for transfers between devices  745 us (48%)
  matrix products  338 us (22%)
  local copies, waits for them, and re-layouts  169 us (11%)
  blocking collectives  164 us (11%)
  other arithmetic  71.6 us (5%)
  starting transfers between devices  24.3 us (2%)
  between operations  21.4 us (1%)
    all_to_all x1, waiting for transfers between devices, on_device(): lax.all_to_all(packed, 'seq', split_axis=3, concat_axis=1, tiled=True)  309 us
    all_to_all x1, waiting for transfers between devices, on_device(): lax.all_to_all(grad_packed_heads, 'seq', split_axis=1, concat_axis=3, til...  228 us
    all_to_all x1, waiting for transfers between devices, on_device(): lax.all_to_all(grad_mixed, 'seq', split_axis=2, concat_axis=1, tiled=True)  89.7 us
    unnamed x1, blocking collectives  85.7 us
    dot_general x3, matrix products, attend_back(): jnp.einsum('hqk,qhd->khd', grad_scores, queries, preferred_element_type=j...  65.7 us
    dot_general x3, matrix products, attend_back(): jnp.einsum('hqk,khd->qhd', grad_scores, key_rows, preferred_element_type=...  65.3 us
    dot_general x4, matrix products, by_columns(): lax.dot_general(former, latter, (((1,), (1,)), ((), ())), preferred_eleme...  55.4 us
    dot_general x4, matrix products, by_rows(): lax.dot_general(former, latter, (((0,), (0,)), ((), ())), preferred_eleme...  51.5 us
  transfers between devices with their start and end apart: 13, of which 7 were waited for; matrix products, arithmetic and copies ran while one was open for 33% of the time, Pallas kernels for 0%

profile of v1, /device:TPU:0, one launch (start us, length us, event | category | flops | bytes accessed | tf_op | source)
XLA Modules:
  0.0 1534.1 jit_solution(8874292483996392261)
XLA Ops:
  17.8 23.3 %all-gather.1 = bf16[16,1,768]{2,1,0:T(2,128)(2,1)S(1)} all-gather(bf16[1,1,768]{2,1,0:T(2,128)(2,1)S(1)} %reshape.303), channel_id=1, replica_groups=mesh['seq'=2,'fsdp'=8,'dp'=2] {'seq','fsdp'}, dimensions={0}, use_global_device_ids=true | all-gather | bytes 26112 | tf_op jit(solution)/shard_map/all_gather | solution.py:144
  42.4 39.8 %all-gather.7.cloned.1.call-done = bf16[1024,3072]{1,0:T(8,128)(2,1)} async-done(((bf16[64,3072]{1,0:T(8,128)(2,1)}), bf16[1024,3072]{1,0:T(8,128)(2,1)}) %all-gather.7.cloned.1.call-update) | async-done | bytes 6291472 | tf_op jit(solution)/shard_map/all_gather | solution.py:142
  82.2 11.2 add_convert_fusion
  93.5 16.3 %reshape.294 = bf16[3,292,3,1024]{3,2,1,0:T(4,128)(2,1)} reshape(bf16[876,3072]{1,0:T(8,128)(2,1)} %add_convert_fusion) | data formatting | bytes 10764288 | tf_op jit(solution)/shard_map/reshape | solution.py:166
  109.8 17.9 %copy.98 = bf16[3,292,3,1024]{1,2,0,3:T(4,128)(2,1)} copy(bf16[3,292,3,1024]{3,2,1,0:T(4,128)(2,1)} %reshape.294) | data formatting | bytes 10764288 | tf_op jit(solution)/shard_map/reshape | solution.py:166
  127.7 7.4 all-to-all-start
  136.4 308.5 %all-to-all-done = bf16[3,292,3,1024]{1,2,0,3:T(4,128)(2,1)} async-done(((bf16[3,292,3,1024]{1,2,0,3:T(4,128)(2,1)}), bf16[3,292,3,1024]{1,2,0,3:T(4,128)(2,1)}, u32[]{:S(2)}, u32[]{:S(2)}) %all-to-all-start) | async-done | bytes 5382176 | tf_op jit(solution)/shard_map/all_to_all | solution.py:167
  444.9 14.8 copy.135
  459.8 14.5 reshape.308
  474.3 34.4 %while.22 = (s32[]{:T(128)}, bf16[3,584,512]{1,2,0:T(8,128)(2,1)S(1)}, f32[3,8,584]{2,1,0:T(8,128)S(1)}, bf16[3,584,3,512]{1,3,2,0:T(8,128)(2,1)}, s32[3,584]{1,0:T(4,128)}, /*index=5*/s32[]{:T(128)}) while((s32[]{:T(128)}, bf16[3,584,512]{1,2,0:T(8,128)(2,1)S(1)}, f32[3,8,584]{2,1,0:T(8,128)S(1)}, bf16[3,584,3,512]{1,3,2,0:T(8,128)(2,1)}, ...), condition=%wide.region_5.6_spmd, body=%wide.region_2.5_spmd.sunk | while | flops 731518976 | bytes 43779996 | solution.py:168
  482.3 3.3 fusion.172
  488.4 2.8 fusion.170
  493.8 3.3 fusion.172
  505.2 3.3 fusion.172
  508.7 3.7 copy.102
  512.4 4.9 all-to-all-start.1
  520.4 42.2 %all-to-all-done.1 = bf16[3,584,512]{2,0,1:T(4,128)(2,1)} async-done(((bf16[3,584,512]{2,0,1:T(4,128)(2,1)}), bf16[3,584,512]{2,0,1:T(4,128)(2,1)}, u32[]{:S(2)}, u32[]{:S(2)}) %all-to-all-start.1) | async-done | bytes 1794080 | tf_op jit(solution)/shard_map/all_to_all | solution.py:169
  569.1 5.3 fusion.109
  576.9 15.2 fusion.90
  592.1 22.1 %convert_reduce_fusion = (f32[4096]{0:T(1024)}, bf16[876,4096]{1,0:T(8,128)(2,1)}) fusion(f32[876,4096]{1,0:T(8,128)} %fusion.90, f32[4096]{0:T(1024)S(1)} %slice.83, bf16[876,1024]{1,0:T(8,128)(2,1)S(1)} %reshape.295, bf16[4096,1024]{1,0:T(8,128)(2,1)} %all-gather.9.cloned.1.call-done), kind=kOutput, calls=%fused_computation.60 | convolution fusion | flops 7430942720 | bytes 31744000 | tf_op jit(solution)/shard_map/dot_general | solution.py:46
  614.2 13.7 multiply_reduce_fusion.3
  633.4 4.4 fusion.113
  637.8 18.0 %fusion.91 = f32[4096,1024]{1,0:T(8,128)} fusion(bf16[876,1024]{1,0:T(8,128)(2,1)S(1)} %reshape.295, f32[876,4096]{1,0:T(8,128)} %fusion.90, f32[4096]{0:T(1024)S(1)} %slice.83), kind=kOutput, calls=%fused_computation.152 | convolution fusion | flops 7384301568 | bytes 32940032 | tf_op jit(solution)/shard_map/dot_general | solution.py:40
  655.9 16.8 %fusion.89 = f32[4096,1024]{1,0:T(8,128)} fusion(bf16[876,4096]{1,0:T(8,128)(2,1)} %get-tuple-element.184, f32[876,1024]{1,0:T(8,128)} %copy-done.6, f32[1024]{0:T(1024)S(1)} %copy-done.47, f32[1024]{0:T(1024)S(1)} %copy-done.34, f32[876]{0:T(1024)S(1)} %fusion.87, f32[876]{0:T(1024)S(1)} %broadcast_multiply_fusion.1), kind=kOutput, calls=%fused_computation.150 | convolution fusion | flops 7352905728 | bytes 27556704 | tf_op jit(solution)/shard_map/dot_general | solution.py:40
  674.2 4.9 convolution_convert_fusion
  680.7 3.9 copy.105
  684.6 4.0 all-to-all-start.2
  688.5 89.7 %all-to-all-done.2 = bf16[3,292,1024]{1,0,2:T(4,128)(2,1)S(1)} async-done(((bf16[3,292,1024]{1,0,2:T(4,128)(2,1)}), bf16[3,292,1024]{1,0,2:T(4,128)(2,1)S(1)}, u32[]{:S(2)}, u32[]{:S(2)}) %all-to-all-start.2) | async-done | bytes 1794080 | tf_op jit(solution)/shard_map/all_to_all | solution.py:198
  778.3 4.2 copy.136
  782.5 5.8 reshape.306
  788.3 187.8 %while.23 = (s32[]{:T(128)}, bf16[3,584,3,512]{1,3,2,0:T(8,128)(2,1)}, bf16[3,584,3,512]{1,3,2,0:T(8,128)(2,1)}, s32[3,584]{1,0:T(4,128)}, f32[3,8,584]{2,1,0:T(8,128)}, /*index=5*/bf16[3,584,512]{1,2,0:T(8,128)(2,1)}, s32[]{:T(128)}) while((s32[]{:T(128)}, bf16[3,584,3,512]{1,3,2,0:T(8,128)(2,1)}, bf16[3,584,3,512]{1,3,2,0:T(8,128)(2,1)}, ...), condition=%wide.region_12.13_spmd, body=%wide.region_10.12_spmd.sunk | while | flops 1824034688 | bytes 138262480 | solution.py:199
  795.0 2.8 fusion.185
  799.3 6.4 fusion.186
  805.7 21.8 %fusion.188 = bf16[8,64,584]{2,1,0:T(8,128)(2,1)S(1)} fusion(bf16[584,8,64]{0,2,1:T(8,128)(2,1)S(1)} %bitcast.146, f32[8,584,584]{1,2,0:T(8,128)} %fusion.186, f32[8,584,584]{1,2,0:T(8,128)} %copy-done, f32[8,584]{1,0:T(8,128)S(1)} %dynamic-slice_bitcast_fusion.8, pred[584]{0:T(1024)(128)(4,1)S(1)} %compare_reduce_fusion.5), kind=kOutput, calls=%fused_computation.38.clone.1 | convolution fusion | flops 379857536 | bytes 23042888 | tf_op jit(solution)/shard_map/while/body/eval_jaxpr/hqk,khd->qhd/dot_general | solution.py:96
  827.5 21.9 %fusion.187 = bf16[8,64,584]{2,1,0:T(8,128)(2,1)S(1)} fusion(bf16[584,8,64]{0,2,1:T(8,128)(2,1)S(1)} %bitcast.144, f32[8,584,584]{1,2,0:T(8,128)} %fusion.186, f32[8,584,584]{1,2,0:T(8,128)} %copy-done, f32[8,584]{1,0:T(8,128)S(1)} %dynamic-slice_bitcast_fusion.8, pred[584]{0:T(1024)(128)(4,1)S(1)} %compare_reduce_fusion.5), kind=kOutput, calls=%fused_computation.37.clone.1 | convolution fusion | flops 379857536 | bytes 23042888 | tf_op jit(solution)/shard_map/while/body/eval_jaxpr/hqk,qhd->khd/dot_general | solution.py:99
  857.5 2.8 fusion.185
  861.8 6.4 fusion.186
  868.2 21.8 %fusion.188 = bf16[8,64,584]{2,1,0:T(8,128)(2,1)S(1)} fusion(bf16[584,8,64]{0,2,1:T(8,128)(2,1)S(1)} %bitcast.146, f32[8,584,584]{1,2,0:T(8,128)} %fusion.186, f32[8,584,584]{1,2,0:T(8,128)} %copy-done, f32[8,584]{1,0:T(8,128)S(1)} %dynamic-slice_bitcast_fusion.8, pred[584]{0:T(1024)(128)(4,1)S(1)} %compare_reduce_fusion.5), kind=kOutput, calls=%fused_computation.38.clone.1 | convolution fusion | flops 379857536 | bytes 23042888 | tf_op jit(solution)/shard_map/while/body/eval_jaxpr/hqk,khd->qhd/dot_general | solution.py:96
  890.0 21.9 %fusion.187 = bf16[8,64,584]{2,1,0:T(8,128)(2,1)S(1)} fusion(bf16[584,8,64]{0,2,1:T(8,128)(2,1)S(1)} %bitcast.144, f32[8,584,584]{1,2,0:T(8,128)} %fusion.186, f32[8,584,584]{1,2,0:T(8,128)} %copy-done, f32[8,584]{1,0:T(8,128)S(1)} %dynamic-slice_bitcast_fusion.8, pred[584]{0:T(1024)(128)(4,1)S(1)} %compare_reduce_fusion.5), kind=kOutput, calls=%fused_computation.37.clone.1 | convolution fusion | flops 379857536 | bytes 23042888 | tf_op jit(solution)/shard_map/while/body/eval_jaxpr/hqk,qhd->khd/dot_general | solution.py:99
  920.0 2.8 fusion.185
  924.3 6.4 fusion.186
  930.7 21.8 %fusion.188 = bf16[8,64,584]{2,1,0:T(8,128)(2,1)S(1)} fusion(bf16[584,8,64]{0,2,1:T(8,128)(2,1)S(1)} %bitcast.146, f32[8,584,584]{1,2,0:T(8,128)} %fusion.186, f32[8,584,584]{1,2,0:T(8,128)} %copy-done, f32[8,584]{1,0:T(8,128)S(1)} %dynamic-slice_bitcast_fusion.8, pred[584]{0:T(1024)(128)(4,1)S(1)} %compare_reduce_fusion.5), kind=kOutput, calls=%fused_computation.38.clone.1 | convolution fusion | flops 379857536 | bytes 23042888 | tf_op jit(solution)/shard_map/while/body/eval_jaxpr/hqk,khd->qhd/dot_general | solution.py:96
  952.5 21.9 %fusion.187 = bf16[8,64,584]{2,1,0:T(8,128)(2,1)S(1)} fusion(bf16[584,8,64]{0,2,1:T(8,128)(2,1)S(1)} %bitcast.144, f32[8,584,584]{1,2,0:T(8,128)} %fusion.186, f32[8,584,584]{1,2,0:T(8,128)} %copy-done, f32[8,584]{1,0:T(8,128)S(1)} %dynamic-slice_bitcast_fusion.8, pred[584]{0:T(1024)(128)(4,1)S(1)} %compare_reduce_fusion.5), kind=kOutput, calls=%fused_computation.37.clone.1 | convolution fusion | flops 379857536 | bytes 23042888 | tf_op jit(solution)/shard_map/while/body/eval_jaxpr/hqk,qhd->khd/dot_general | solution.py:99
  976.1 13.4 copy.110
  989.5 6.7 all-to-all-start.3
  999.9 228.1 %all-to-all-done.3 = bf16[3,584,3,512]{3,2,0,1:T(4,128)(2,1)} async-done(((bf16[3,584,3,512]{3,2,0,1:T(4,128)(2,1)}), bf16[3,584,3,512]{3,2,0,1:T(4,128)(2,1)}, u32[]{:S(2)}, u32[]{:S(2)}) %all-to-all-start.3) | async-done | bytes 5382176 | tf_op jit(solution)/shard_map/all_to_all | solution.py:200
  1228.1 4.7 convert_reduce_fusion.1
  1232.8 9.7 copy.112
  1242.5 12.9 reshape.298
  1255.4 12.3 fusion.112
  1270.2 17.4 %add_add_fusion.3 = f32[876,1024]{1,0:T(8,128)} fusion(f32[876,1024]{1,0:T(8,128)} %copy-done.6, f32[1024]{0:T(1024)S(1)} %copy-done.46, bf16[4096,1024]{1,0:T(8,128)(2,1)} %all-gather.9.cloned.1.call-done, f32[876,4096]{1,0:T(8,128)} %fusion.90, f32[4096]{0:T(1024)S(1)} %copy-done.42), kind=kOutput, calls=%fused_computation.73 | convolution fusion | flops 7386095616 | bytes 29937664 | tf_op jit(solution)/shard_map/dot_general | solution.py:36
  1287.6 4.0 reshape.299
  1291.7 13.2 multiply_reduce_fusion.2
  1305.0 85.7 %all-reduce = bf16[12288]{0:T(1024)(128)(2,1)S(1)} all-reduce(f32[12288]{0:T(1024)S(1)} %constant_dynamic-update-slice_fusion.1), channel_id=7, replica_groups=mesh['seq'=2,'fsdp'=8,'dp'=2] {'seq','fsdp'}, use_global_device_ids=true, to_apply=%region_33.34.clone | all-reduce | flops 12288 | bytes 73728
  1390.8 5.3 psum.38
  1396.1 6.2 fusion.92
  1408.7 5.7 add_add_fusion.2
  1414.4 6.3 reduce-scatter.5.cloned.1.call-done
  1422.0 15.3 all-gather
  1438.4 30.4 %all-reduce.4.cloned.1.call-done = (bf16[64,1024]{1,0:T(8,128)(2,1)}, bf16[256,1024]{1,0:T(8,128)(2,1)}, bf16[256,1024]{1,0:T(8,128)(2,1)}) async-done(((bf16[64,1024]{1,0:T(8,128)(2,1)}, bf16[256,1024]{1,0:T(8,128)(2,1)}, bf16[256,1024]{1,0:T(8,128)(2,1)}), (bf16[64,1024]{1,0:T(8,128)(2,1)}, bf16[256,1024]{1,0:T(8,128)(2,1)}, bf16[256,1024]{1,0:T(8,128)(2,1)})) %all-reduce.4.cloned.1.call-update) | async-done | bytes 1179664 | tf_op jit(solution)/shard_map/psum | solution.py:235
  1477.4 3.7 reshape.300
  1481.2 33.9 %psum.39 = f32[]{:T(128)} all-reduce(f32[]{:T(128)S(6)} %add.244), channel_id=1, replica_groups=mesh['seq'=2,'fsdp'=8,'dp'=2] {'seq','fsdp'}, use_global_device_ids=true, to_apply=%region_36.37 | all-reduce | flops 1 | bytes 8 | tf_op jit(solution)/shard_map/psum | solution.py:248
  1519.1 3.4 fusion.101
  1522.5 3.7 fusion.95
  (243 shorter events, 105.8 us)
Async XLA Ops:
  7.2 6.7 copy-start.2
  7.2 75.0 %all-gather.7.cloned.1.call-start = ((), (), s32[]{:S(2)}) async-start(), calls=%async_computation.8 | async-start | bytes 6684672 | tf_op jit(solution)/shard_map/all_gather | solution.py:142
  9.3 559.8 %all-gather.11.cloned.1.call-start = ((), (), s32[]{:S(2)}) async-start(), calls=%async_computation.10 | async-start | bytes 2228224 | tf_op jit(solution)/shard_map/all_gather | solution.py:143
  11.0 565.8 %all-gather.13.cloned.1.call-start = ((), (), s32[]{:S(2)}) async-start(), calls=%async_computation.11 | async-start | bytes 8912896 | tf_op jit(solution)/shard_map/all_gather | solution.py:147
  16.4 77.1 %copy-start.25 = (f32[3,292]{1,0:T(4,128)}, f32[3,292]{1,0:T(4,128)S(1)}, u32[]{:S(2)}) copy-start(f32[3,292]{1,0:T(4,128)S(1)} %broadcast_multiply_fusion) | copy-start | bytes 10516
  16.5 77.0 %copy-start.35 = (f32[876]{0:T(1024)}, f32[876]{0:T(1024)S(1)}, u32[]{:S(2)}) copy-start(f32[876]{0:T(1024)S(1)} %div.108) | copy-start | bytes 10516
  17.8 23.4 %copy-start.31 = (f32[876]{0:T(1024)}, f32[876]{0:T(1024)S(1)}, u32[]{:S(2)}) copy-start(f32[876]{0:T(1024)S(1)} %add.225) | copy-start | bytes 10516
  17.8 75.7 %copy-start.37 = (f32[876]{0:T(1024)}, f32[876]{0:T(1024)S(1)}, u32[]{:S(2)}) copy-start(f32[876]{0:T(1024)S(1)} %rsqrt.26) | copy-start | bytes 10516
  42.4 51.1 %copy-start.27 = (f32[1024]{0:T(1024)}, f32[1024]{0:T(1024)S(1)}, u32[]{:S(2)}) copy-start(f32[1024]{0:T(1024)S(1)} %get-tuple-element.206) | copy-start | bytes 12292
  42.4 51.1 %copy-start.44 = (f32[1024]{0:T(1024)}, f32[1024]{0:T(1024)S(1)}, u32[]{:S(2)}) copy-start(f32[1024]{0:T(1024)S(1)} %get-tuple-element.205) | copy-start | bytes 12292
  127.7 7.8 copy-start.10
  127.7 317.2 %all-to-all-start = ((bf16[3,292,3,1024]{1,2,0,3:T(4,128)(2,1)}), bf16[3,292,3,1024]{1,2,0,3:T(4,128)(2,1)}, u32[]{:S(2)}, u32[]{:S(2)}) async-start(bf16[3,292,3,1024]{1,2,0,3:T(4,128)(2,1)} %copy.98), calls=%async_computation | async-start | bytes 18874368 | tf_op jit(solution)/shard_map/all_to_all | solution.py:167
  135.2 456.9 %all-gather.9.cloned.1.call-start = ((), (), s32[]{:S(2)}) async-start(), calls=%async_computation.9 | async-start | bytes 8912896 | tf_op jit(solution)/shard_map/all_gather | solution.py:148
  508.7 11.6 copy-start.24
  512.4 50.1 %all-to-all-start.1 = ((bf16[3,584,512]{2,0,1:T(4,128)(2,1)}), bf16[3,584,512]{2,0,1:T(4,128)(2,1)}, u32[]{:S(2)}, u32[]{:S(2)}) async-start(bf16[3,584,512]{2,0,1:T(4,128)(2,1)} %copy.102), calls=%async_computation.1 | async-start | bytes 4784128 | tf_op jit(solution)/shard_map/all_to_all | solution.py:169
  517.4 884.9 %reduce-scatter.7.cloned.1.call-start = ((), (), s32[]{:S(2)}) async-start(), calls=%async_computation.13 | async-start | bytes 4456448 | tf_op jit(solution)/shard_map/reduce_scatter | solution.py:226
  518.7 119.1 %copy-start.41 = (f32[4096]{0:T(1024)}, f32[4096]{0:T(1024)S(1)}, u32[]{:S(2)}) copy-start(f32[4096]{0:T(1024)S(1)} %slice.83) | copy-start | bytes 49156
  520.3 117.5 %copy-start.4 = (bf16[876,1024]{1,0:T(8,128)(2,1)}, bf16[876,1024]{1,0:T(8,128)(2,1)S(1)}, u32[]{:S(2)}) copy-start(bf16[876,1024]{1,0:T(8,128)(2,1)S(1)} %reshape.295) | copy-start | bytes 5382148
  564.6 4.5 copy-start.48
  569.1 7.7 copy-start.34
  569.1 7.7 copy-start.47
  592.1 22.1 %copy-start.7 = (f32[876,1024]{1,0:T(8,128)S(1)}, f32[876,1024]{1,0:T(8,128)}, u32[]{:S(2)}) copy-start(f32[876,1024]{1,0:T(8,128)} %copy-done.6) | copy-start | bytes 10764292
  629.0 1.8 copy-start.1
  629.1 4.3 copy-start.17
  629.1 3.1 copy-start.29
  637.7 766.2 %reduce-scatter.11.cloned.1.call-start = ((), (), s32[]{:S(2)}) async-start(), calls=%async_computation.15 | async-start | bytes 17825792 | tf_op jit(solution)/shard_map/reduce_scatter | solution.py:231
  655.9 750.1 %reduce-scatter.9.cloned.1.call-start = ((), (), s32[]{:S(2)}) async-start(), calls=%async_computation.14 | async-start | bytes 17825792 | tf_op jit(solution)/shard_map/reduce_scatter | solution.py:230
  684.6 93.7 %all-to-all-start.2 = ((bf16[3,292,1024]{1,0,2:T(4,128)(2,1)}), bf16[3,292,1024]{1,0,2:T(4,128)(2,1)S(1)}, u32[]{:S(2)}, u32[]{:S(2)}) async-start(bf16[3,292,1024]{1,0,2:T(4,128)(2,1)} %copy.105), calls=%async_computation.2 | async-start | bytes 6291456 | tf_op jit(solution)/shard_map/all_to_all | solution.py:198
  795.0 4.3 copy-start
  857.5 4.3 copy-start
  920.0 4.3 copy-start
  989.5 6.8 copy-start.3
  989.5 6.8 copy-start.26
  989.5 6.8 copy-start.28
  989.5 6.8 copy-start.33
  989.5 6.8 copy-start.45
  989.5 238.6 %all-to-all-start.3 = ((bf16[3,584,3,512]{3,2,0,1:T(4,128)(2,1)}), bf16[3,584,3,512]{3,2,0,1:T(4,128)(2,1)}, u32[]{:S(2)}, u32[]{:S(2)}) async-start(bf16[3,584,3,512]{3,2,0,1:T(4,128)(2,1)} %copy.110), calls=%async_computation.3 | async-start | bytes 14352384 | tf_op jit(solution)/shard_map/all_to_all | solution.py:200
  996.2 424.5 %reduce-scatter.5.cloned.1.call-start = ((), (), s32[]{:S(2)}) async-start(), calls=%async_computation.12 | async-start | bytes 13369344 | tf_op jit(solution)/shard_map/reduce_scatter | solution.py:225
  1267.7 2.1 copy-start.8
  1267.7 2.5 copy-start.42
  1267.7 2.5 copy-start.46
  1267.7 201.1 %all-reduce.4.cloned.1.call-start = ((), (), s32[]{:S(2)}) async-start(), calls=%async_computation.16 | async-start | bytes 2359296 | tf_op jit(solution)/shard_map/psum | solution.py:235
  1287.6 4.0 copy-start.36
  1287.6 4.0 copy-start.38
  1291.6 13.3 copy-start.39
  1291.6 13.3 copy-start.50
  1291.6 13.3 copy-start.49
  1291.7 13.3 copy-start.40
  1291.7 104.4 %copy-start.32 = (f32[876]{0:T(1024)S(1)}, f32[876]{0:T(1024)}, u32[]{:S(2)}) copy-start(f32[876]{0:T(1024)} %copy-done.31) | copy-start | bytes 10516
  1396.1 12.6 copy-start.5
  1396.1 12.6 copy-start.30
  1421.9 93.9 %copy-start.43 = (f32[768]{0:T(1024)S(1)}, f32[768]{0:T(1024)}, u32[]{:S(2)}) copy-start(f32[768]{0:T(1024)} %param.31) | copy-start | bytes 9220
  1422.0 93.9 %copy-start.51 = (f32[768]{0:T(1024)S(1)}, f32[768]{0:T(1024)}, u32[]{:S(2)}) copy-start(f32[768]{0:T(1024)} %param.41) | copy-start | bytes 9220
  1422.0 93.9 %copy-start.52 = (f32[768]{0:T(1024)S(1)}, f32[768]{0:T(1024)}, u32[]{:S(2)}) copy-start(f32[768]{0:T(1024)} %param.36) | copy-start | bytes 9220
  1422.0 94.6 %copy-start.18 = (f32[64,1024]{1,0:T(8,128)S(1)}, f32[64,1024]{1,0:T(8,128)}, u32[]{:S(2)}) copy-start(f32[64,1024]{1,0:T(8,128)} %param.28) | copy-start | bytes 786436
  1437.6 81.5 %copy-start.12 = (f32[64,3072]{1,0:T(8,128)S(1)}, f32[64,3072]{1,0:T(8,128)}, u32[]{:S(2)}) copy-start(f32[64,3072]{1,0:T(8,128)} %param.27) | copy-start | bytes 2359300
  1481.2 41.3 %copy-start.9 = (f32[256,1024]{1,0:T(8,128)S(1)}, f32[256,1024]{1,0:T(8,128)}, u32[]{:S(2)}) copy-start(f32[256,1024]{1,0:T(8,128)} %param.29) | copy-start | bytes 3145732
  1481.2 41.3 %copy-start.11 = (f32[256,1024]{1,0:T(8,128)S(1)}, f32[256,1024]{1,0:T(8,128)}, u32[]{:S(2)}) copy-start(f32[256,1024]{1,0:T(8,128)} %param.30) | copy-start | bytes 3145732
  1515.9 6.6 copy-start.13
  1515.9 6.6 copy-start.14
  1515.9 6.6 copy-start.19
  1515.9 6.6 copy-start.20
  1515.9 6.6 copy-start.21
  1516.0 6.6 copy-start.22
  (5 other events, 6.1 us)
Sparse Core Ops, SparseCore 0:
  10.9 71.2 all-gather.6
  85.1 40.6 all-gather.10
  128.7 207.7 all-gather.12
  339.2 107.4 all-gather.8
  637.9 110.9 reduce-scatter.6
  751.0 188.6 reduce-scatter.10
  942.0 336.6 reduce-scatter.8
  1283.4 137.3 reduce-scatter.4
  1424.0 44.7 all-reduce.3
